TPU v7x, 256 devices: a whole 4x4x8 slice. The times are simulated.
256 devices in a mesh: gx: 16 (over z, y_lo), gz: 8 (over y_hi, x), ta: 2 (over core).
Axes of the slice: x: 4, y: 4 (y_hi: 2, y_lo: 2; y = y_hi * 2 + y_lo), z: 8, core: 2. Of those that a mesh axis runs over, the one named last changes fastest.
Arguments:
- fine_field: bfloat16 [2, 2, 6, 4, 262144], P(None, None, None, None, ('gx', 'gz', 'ta')), may hold values from -6 to 6
- null_vectors: bfloat16 [2, 2, 6, 32, 262144], P(None, None, None, None, ('gx', 'gz', 'ta')), may hold values from -0.21875 to 0.21875
- aggregate: int32 [262144], P(('gx', 'gz', 'ta')), may hold values from 0 to 255
- coarse_links: bfloat16 [32, 2, 16, 4, 9, 64, 128], P('gx', None, 'gz', 'ta'), may hold values from -0.1875 to 0.1875
Outputs:
- prolonged: bfloat16 [2, 2, 6, 4, 262144], P(None, None, None, None, ('gx', 'gz', 'ta'))
All inputs are finite; a program needn't handle non-finite values.
Results may differ from a plain program's by a relative error of at most 0.0064.
Values may be sent and summed in bfloat16 or wider, within the bound.
A program may use at most 128 MiB of HBM per device.

v0:
```python
import functools

import jax
import jax.numpy as jnp
from jax import lax
from jax.experimental import pallas as pl
from jax.experimental.pallas import tpu as pltpu
from jax.sharding import PartitionSpec as P

RHS = 4
NV = 32
SC = 6
SITES = 16
LANES = 128
CHUNKS = 2
PER = RHS // CHUNKS
F32 = jnp.float32
BF16 = jnp.bfloat16
NT = (((1,), (1,)), ((), ()))
TN = (((0,), (0,)), ((), ()))


def ring_order(count):
    long = count // 2
    pairs = [(dz, dy) for dz in range(long) for dy in range(2) if (dz, dy) != (0, 0)]
    return sorted(pairs, key=lambda p: -(2 * min(p[0], long - p[0]) + p[1]))


def site_bits(s):
    return (s >> 3) & 1, (s >> 2) & 1, (s >> 1) & 1, s & 1


def site_of(x, y, z, t):
    return ((x * 2 + y) * 2 + z) * 2 + t


def local_terms(s):
    x, y, z, t = site_bits(s)
    return (
        (0, s),
        (1, site_of(x, 1 - y, z, t)),
        (2, site_of(x, 1 - y, z, t)),
        (3 if x == 0 else 4, site_of(1 - x, y, z, t)),
        (5 if z == 0 else 6, site_of(x, y, 1 - z, t)),
        (7 if t == 0 else 8, site_of(x, y, z, 1 - t)),
    )


def remote_terms(s):
    x, y, z, t = site_bits(s)
    return (
        (3, 0, site_of(0, y, z, t)) if x == 1 else (4, 1, site_of(1, y, z, t)),
        (5, 2, site_of(x, y, 0, t)) if z == 1 else (6, 3, site_of(x, y, 1, t)),
        (7, 4, site_of(x, y, z, 0)) if t == 1 else (8, 4, site_of(x, y, z, 1)),
    )


def kernel(
    nx,
    nz,
    agg_hbm,
    field_hbm,
    vec_hbm,
    links_hbm,
    out_hbm,
    agg,
    field,
    field32,
    vec,
    links,
    hot,
    rows,
    part32,
    part,
    got,
    spread,
    faces,
    blocks,
    packed,
    whole,
    picked,
    out32,
    out,
    in_sem,
    out_sem,
    rs_send,
    rs_recv,
    face_send,
    face_recv,
    ag_send,
    ag_recv,
):
    fine = agg.shape[1]
    tiles = fine // LANES
    me = lax.axis_index("gx")
    my_z = lax.axis_index("gz")
    my_t = lax.axis_index("ta")
    order = ring_order(nx)
    long = nx // 2

    loads = [
        pltpu.make_async_copy(agg_hbm, agg, in_sem.at[0]),
        pltpu.make_async_copy(field_hbm, field, in_sem.at[1]),
        pltpu.make_async_copy(vec_hbm.at[:, 0], vec.at[:, 0], in_sem.at[2]),
        pltpu.make_async_copy(vec_hbm.at[:, 1], vec.at[:, 1], in_sem.at[3]),
        pltpu.make_async_copy(links_hbm, links, in_sem.at[4]),
    ]
    for load in loads:
        load.start()

    def member(dz, dy):
        z = lax.rem(lax.div(me, 2) + dz, long)
        y = lax.rem(lax.rem(me, 2) + dy, 2)
        return z * 2 + y

    barrier = pltpu.get_barrier_semaphore()
    neighbours = [
        {"gx": lax.rem(me + 1, nx)},
        {"gx": lax.rem(me + nx - 1, nx)},
        {"gz": lax.rem(my_z + 1, nz)},
        {"gz": lax.rem(my_z + nz - 1, nz)},
        {"ta": 1 - my_t},
    ]
    greeted = [{"gx": member(dz, dy)} for dz, dy in order] + neighbours[2:]
    for device in greeted:
        pl.semaphore_signal(barrier, inc=1, device_id=device, device_id_type=pl.DeviceIdType.MESH)

    loads[0].wait()
    groups = hot.shape[0]

    def hot_tile(i, carry):
        lanes = pl.ds(pl.multiple_of(i * LANES, LANES), LANES)
        site = lax.broadcasted_iota(jnp.int32, (groups, LANES), 0)
        hot[:, lanes] = jnp.where(site == agg[:, lanes], 1.0, 0.0).astype(BF16)
        return carry

    lax.fori_loop(0, tiles, hot_tile, 0)

    loads[1].wait()
    for ri in range(2):
        for chi in range(2):
            for a in range(SC):
                plane = (ri * 2 + chi) * SC + a
                field32[plane, :, :] = field[ri, chi, a].astype(F32)
    loads[2].wait()
    loads[3].wait()

    sends = []
    for c in range(CHUNKS):

        def project(step, carry, c=c):
            chi = lax.div(step, tiles)
            lanes = pl.ds(pl.multiple_of(lax.rem(step, tiles) * LANES, LANES), LANES)
            real = [jnp.zeros((NV, LANES), F32) for _ in range(PER)]
            imag = [jnp.zeros((NV, LANES), F32) for _ in range(PER)]
            for a in range(SC):
                vr = vec[0, chi, a, :, lanes].astype(F32)
                vi = vec[1, chi, a, :, lanes].astype(F32)
                for j in range(PER):
                    r = c * PER + j
                    fr = field32[chi * SC + a, r : r + 1, lanes]
                    fi = field32[(2 + chi) * SC + a, r : r + 1, lanes]
                    real[j] = real[j] + (vr * fr + vi * fi)
                    imag[j] = imag[j] + (vr * fi - vi * fr)
            for j in range(PER):
                base = pl.multiple_of(chi * NV, NV)
                rows[pl.ds(j * LANES + base, NV), lanes] = real[j].astype(BF16)
                rows[pl.ds(j * LANES + 2 * NV + base, NV), lanes] = imag[j].astype(BF16)
            return carry

        lax.fori_loop(0, 2 * tiles, project, 0)
        sums = lax.dot_general(hot[...], rows[...], NT, preferred_element_type=F32)
        part32[c] = sums
        part[c] = sums.astype(BF16)
        if c == 0:
            pl.semaphore_wait(barrier, len(greeted))
        for i, (dz, dy) in enumerate(order):
            peer = member(dz, dy)
            copy = pltpu.make_async_remote_copy(
                src_ref=part.at[c, pl.ds(pl.multiple_of(peer * SITES, SITES), SITES)],
                dst_ref=got.at[c, i],
                send_sem=rs_send.at[c, i],
                recv_sem=rs_recv.at[c, i],
                device_id={"gx": peer},
                device_id_type=pl.DeviceIdType.MESH,
            )
            copy.start()
            sends.append(copy)

    lane = lax.broadcasted_iota(jnp.int32, (8, LANES), 1)
    low = lane < LANES // 2
    low16 = lax.broadcasted_iota(jnp.int32, (SITES, LANES), 1) < LANES // 2
    upper = lax.broadcasted_iota(jnp.int32, (8, LANES), 0) < RHS
    half = LANES // 2

    def expand(values, slot):
        for r in range(RHS):
            v = values[r]
            spread[slot, r * SITES : (r + 1) * SITES, :] = jnp.where(low16, v, -v)
            spread[slot, (RHS + r) * SITES : (RHS + r + 1) * SITES, :] = pltpu.roll(v, half, 1)

    def site_rows(slot, s):
        return spread[slot, pl.ds(s, 2 * RHS, stride=SITES), :]

    def send_faces(k):
        copies = []
        for i, back in enumerate((1, 0, 3, 2, 4)):
            copy = pltpu.make_async_remote_copy(
                src_ref=blocks.at[k],
                dst_ref=faces.at[k, back],
                send_sem=face_send.at[k, i],
                recv_sem=face_recv.at[k, back],
                device_id=neighbours[i],
                device_id_type=pl.DeviceIdType.MESH,
            )
            copy.start()
            copies.append(copy)
        return copies

    def term_product(group, terms):
        total = None
        count = len(terms[0])
        for first in range(0, count, 2):
            pick = range(first, min(first + 2, count))
            left = [jnp.concatenate([terms[j][m][1] for j in range(4)], axis=0).astype(BF16) for m in pick]
            right = []
            for m in pick:
                part_links = []
                for j in range(4):
                    x, y, z, t = site_bits(group * 4 + j)
                    part_links.append(links[x, y, z, t, terms[j][m][0]])
                right.append(jnp.concatenate(part_links, axis=0))
            lhs = left[0] if len(left) == 1 else jnp.concatenate(left, axis=1)
            rhs = right[0] if len(right) == 1 else jnp.concatenate(right, axis=1)
            product = lax.dot_general(lhs, rhs, NT, preferred_element_type=F32)
            total = product if total is None else total + product
        return total

    def apply_operator(k, sites):
        copies = send_faces(k)
        totals = []
        for group in range(4):
            terms = [[(m, sites[n]) for m, n in local_terms(group * 4 + j)] for j in range(4)]
            totals.append(term_product(group, terms))
        for slot in range(5):
            copies[(1, 0, 3, 2, 4)[slot]].wait_recv()
            expand([faces[k, slot, r].astype(F32) for r in range(RHS)], slot)
        result = []
        for group in range(4):
            terms = [
                [(m, site_rows(slot, n)) for m, slot, n in remote_terms(group * 4 + j)] for j in range(4)
            ]
            total = totals[group] + term_product(group, terms)
            for j in range(4):
                block = total[8 * j : 8 * j + 8, LANES * (j // 2) : LANES * (j // 2) + LANES]
                swapped = pltpu.roll(block, RHS, 0)
                signed = jnp.where(upper, -swapped, swapped)
                if j % 2 == 0:
                    new = jnp.where(low, block, pltpu.roll(signed, half, 1))
                else:
                    new = jnp.where(low, pltpu.roll(block, half, 1), signed)
                new = new.astype(BF16).astype(F32)
                s = group * 4 + j
                kept = jnp.where(low, new, -new)
                packed[pl.ds(s, RHS, stride=SITES), :] = kept[:RHS]
                result.append(new)
        for r in range(RHS):
            blocks[k + 1, r] = packed[r * SITES : (r + 1) * SITES, :].astype(BF16)
        return result, copies

    mine = pl.ds(pl.multiple_of(me * SITES, SITES), SITES)
    values = []
    loads[4].wait()
    for c in range(CHUNKS):
        total = part32[c, mine, :]
        for i in range(len(order)):
            sends[c * len(order) + i].wait_recv()
            total = total + got[c, i].astype(F32)
        for j in range(PER):
            rounded = total[:, j * LANES : (j + 1) * LANES].astype(BF16)
            blocks[0, c * PER + j] = rounded
            values.append(rounded.astype(F32))
    expand(values, 5)
    sites = [site_rows(5, s) for s in range(SITES)]
    sites, faces_a = apply_operator(0, sites)
    sites, faces_b = apply_operator(1, sites)

    gathers = []
    for c in range(CHUNKS):
        for i, (dz, dy) in enumerate(order):
            copy = pltpu.make_async_remote_copy(
                src_ref=blocks.at[2, pl.ds(c * PER, PER)],
                dst_ref=whole.at[pl.ds(c * PER, PER), mine],
                send_sem=ag_send.at[c, i],
                recv_sem=ag_recv.at[c, i],
                device_id={"gx": member(dz, dy)},
                device_id_type=pl.DeviceIdType.MESH,
            )
            copy.start()
            gathers.append(copy)
    for r in range(RHS):
        whole[r, mine, :] = blocks[2, r]

    for c in range(CHUNKS):
        for i in range(len(order)):
            gathers[c * len(order) + i].wait_recv()
        for j in range(PER):
            picked[j] = lax.dot_general(whole[c * PER + j], hot[...], TN, preferred_element_type=F32)

        def prolong(step, carry, c=c):
            chi = lax.div(step, tiles)
            lanes = pl.ds(pl.multiple_of(lax.rem(step, tiles) * LANES, LANES), LANES)
            base = pl.multiple_of(chi * NV, NV)
            pr = [picked[j, pl.ds(base, NV), lanes] for j in range(PER)]
            pi = [picked[j, pl.ds(2 * NV + base, NV), lanes] for j in range(PER)]
            for a in range(SC):
                vr = vec[0, chi, a, :, lanes].astype(F32)
                vi = vec[1, chi, a, :, lanes].astype(F32)
                for j in range(PER):
                    r = c * PER + j
                    real = jnp.sum(vr * pr[j] - vi * pi[j], axis=0, keepdims=True)
                    imag = jnp.sum(vr * pi[j] + vi * pr[j], axis=0, keepdims=True)
                    out32[chi * SC + a, r : r + 1, lanes] = real
                    out32[(2 + chi) * SC + a, r : r + 1, lanes] = imag
            return carry

        lax.fori_loop(0, 2 * tiles, prolong, 0)

    for ri in range(2):
        for chi in range(2):
            for a in range(SC):
                out[ri, chi, a] = out32[(ri * 2 + chi) * SC + a].astype(BF16)
    store = pltpu.make_async_copy(out, out_hbm, out_sem)
    store.start()
    for copy in sends + faces_a + faces_b + gathers:
        copy.wait_send()
    store.wait()


def per_device(fine_field, null_vectors, aggregate, coarse_links):
    nx = lax.axis_size("gx")
    nz = lax.axis_size("gz")
    fine = fine_field.shape[-1]
    groups = SITES * nx
    peers = nx - 1
    width = PER * LANES
    anywhere = pl.BlockSpec(memory_space=pl.ANY)
    dma = pltpu.SemaphoreType.DMA
    return pl.pallas_call(
        functools.partial(kernel, nx, nz),
        out_shape=jax.ShapeDtypeStruct(fine_field.shape, BF16),
        in_specs=[anywhere] * 4,
        out_specs=anywhere,
        scratch_shapes=[
            pltpu.VMEM((1, fine), jnp.int32),
            pltpu.VMEM(fine_field.shape, BF16),
            pltpu.VMEM((4 * SC, RHS, fine), F32),
            pltpu.VMEM(null_vectors.shape, BF16),
            pltpu.VMEM(coarse_links.shape, BF16),
            pltpu.VMEM((groups, fine), BF16),
            pltpu.VMEM((width, fine), BF16),
            pltpu.VMEM((CHUNKS, groups, width), F32),
            pltpu.VMEM((CHUNKS, groups, width), BF16),
            pltpu.VMEM((CHUNKS, peers, SITES, width), BF16),
            pltpu.VMEM((6, 2 * RHS * SITES, LANES), F32),
            pltpu.VMEM((2, 5, RHS, SITES, LANES), BF16),
            pltpu.VMEM((3, RHS, SITES, LANES), BF16),
            pltpu.VMEM((RHS * SITES, LANES), F32),
            pltpu.VMEM((RHS, groups, LANES), BF16),
            pltpu.VMEM((PER, LANES, fine), F32),
            pltpu.VMEM((4 * SC, RHS, fine), F32),
            pltpu.VMEM(fine_field.shape, BF16),
            dma((5,)),
            dma,
            dma((CHUNKS, peers)),
            dma((CHUNKS, peers)),
            dma((2, 5)),
            dma((2, 5)),
            dma((CHUNKS, peers)),
            dma((CHUNKS, peers)),
        ],
        compiler_params=pltpu.CompilerParams(
            collective_id=0, has_side_effects=True, vmem_limit_bytes=48 * 1024 * 1024
        ),
        name="coarse_cycle",
    )(aggregate.reshape(1, fine), fine_field, null_vectors, coarse_links)


def solution(mesh):
    in_specs = (
        P(None, None, None, None, ("gx", "gz", "ta")),
        P(None, None, None, None, ("gx", "gz", "ta")),
        P(("gx", "gz", "ta")),
        P("gx", None, "gz", "ta", None, None, None),
    )
    out_specs = P(None, None, None, None, ("gx", "gz", "ta"))
    return jax.shard_map(per_device, mesh=mesh, in_specs=in_specs, out_specs=out_specs, check_vma=False)
```

profile of v0, /device:TPU:8, one launch (start us, length us, event | category | flops | bytes accessed | tf_op | source)
XLA Modules:
  0.0 43.4 jit_solution(14452900491633438161)
XLA Ops:
  0.0 0.0 copy-start
  0.0 1.7 %copy-done = bf16[2,2,2,2,9,64,128]{6,5,4,3,2,1,0:T(8,128)(2,1)S(1)} copy-done((bf16[2,2,2,2,9,64,128]{6,5,4,3,2,1,0:T(8,128)(2,1)S(1)}, bf16[2,2,2,2,9,64,128]{6,5,4,3,2,1,0:T(8,128)(2,1)}, u32[]{:S(2)}) %copy-start) | copy-done | bytes 2359320
  1.7 0.0 copy-start.1
  1.7 1.4 %copy-done.1 = bf16[2,2,6,32,1024]{4,3,2,1,0:T(8,128)(2,1)S(1)} copy-done((bf16[2,2,6,32,1024]{4,3,2,1,0:T(8,128)(2,1)S(1)}, bf16[2,2,6,32,1024]{4,3,2,1,0:T(8,128)(2,1)}, u32[]{:S(2)}) %copy-start.1) | copy-done | bytes 1572888
  3.1 0.0 copy-start.2
  3.1 0.9 %copy-done.2 = bf16[2,2,6,4,1024]{4,3,2,1,0:T(4,128)(2,1)S(1)} copy-done((bf16[2,2,6,4,1024]{4,3,2,1,0:T(4,128)(2,1)S(1)}, bf16[2,2,6,4,1024]{4,3,2,1,0:T(4,128)(2,1)}, u32[]{:S(2)}) %copy-start.2) | copy-done | bytes 196632
  4.0 0.0 copy-start.3
  4.0 0.7 %copy-done.3 = s32[1024]{0:T(1024)S(1)} copy-done((s32[1024]{0:T(1024)S(1)}, s32[1024]{0:T(1024)}, u32[]{:S(2)}) %copy-start.3) | copy-done | bytes 4120
  4.7 38.0 %coarse_cycle.1 = bf16[2,2,6,4,1024]{4,3,2,1,0:T(4,128)(2,1)S(1)} custom-call(s32[1,1024]{1,0:T(1,128)S(1)} %bitcast.1, bf16[2,2,6,4,1024]{4,3,2,1,0:T(4,128)(2,1)S(1)} %copy-done.2, bf16[2,2,6,32,1024]{4,3,2,1,0:T(8,128)(2,1)S(1)} %copy-done.1, bf16[2,2,2,2,9,64,128]{6,5,4,3,2,1,0:T(8,128)(2,1)S(1)} %copy-done), custom_call_target="tpu_custom_call" | custom-call | tf_op jit(solution)/shard_map/coarse_cycle/pallas_call | solution.py:349
  42.7 0.7 %copy.6 = bf16[2,2,6,4,1024]{4,3,2,1,0:T(4,128)(2,1)} copy(bf16[2,2,6,4,1024]{4,3,2,1,0:T(4,128)(2,1)S(1)} %coarse_cycle.1) | data formatting | bytes 393216
Async XLA Ops:
  0.0 1.7 %copy-start = (bf16[2,2,2,2,9,64,128]{6,5,4,3,2,1,0:T(8,128)(2,1)S(1)}, bf16[2,2,2,2,9,64,128]{6,5,4,3,2,1,0:T(8,128)(2,1)}, u32[]{:S(2)}) copy-start(bf16[2,2,2,2,9,64,128]{6,5,4,3,2,1,0:T(8,128)(2,1)} %links_hbm.1) | copy-start | bytes 7077892
  1.7 1.4 %copy-start.1 = (bf16[2,2,6,32,1024]{4,3,2,1,0:T(8,128)(2,1)S(1)}, bf16[2,2,6,32,1024]{4,3,2,1,0:T(8,128)(2,1)}, u32[]{:S(2)}) copy-start(bf16[2,2,6,32,1024]{4,3,2,1,0:T(8,128)(2,1)} %vec_hbm.1) | copy-start | bytes 4718596
  3.1 0.9 %copy-start.2 = (bf16[2,2,6,4,1024]{4,3,2,1,0:T(4,128)(2,1)S(1)}, bf16[2,2,6,4,1024]{4,3,2,1,0:T(4,128)(2,1)}, u32[]{:S(2)}) copy-start(bf16[2,2,6,4,1024]{4,3,2,1,0:T(4,128)(2,1)} %field_hbm.1) | copy-start | bytes 589828
  4.0 0.7 %copy-start.3 = (s32[1024]{0:T(1024)S(1)}, s32[1024]{0:T(1024)}, u32[]{:S(2)}) copy-start(s32[1024]{0:T(1024)} %param.6) | copy-start | bytes 12292
where the time goes:
time: 43.6 us; the launch traced here: 43.4 us
  Pallas kernels  38 us (87%)
  local copies, waits for them, and re-layouts  5.36 us (12%)
    pallas_call x1, Pallas kernels, per_device(): pl.pallas_call(functools.partial(kernel, nx, nz), out_shape=jax.ShapeDtyp...  38 us
    unnamed x9, local copies, waits for them, and re-layouts  5.36 us

commit v1 on v0

--- a/solution.py
+++ b/solution.py
@@ -90,6 +90,9 @@
     ag_send,
     ag_recv,
 ):
+    def await_bytes(ref, sem):
+        pltpu.make_async_copy(ref, ref, sem).wait()
+
     fine = agg.shape[1]
     tiles = fine // LANES
     me = lax.axis_index("gx")
@@ -145,7 +148,6 @@
     loads[2].wait()
     loads[3].wait()
 
-    sends = []
     for c in range(CHUNKS):
 
         def project(step, carry, c=c):
@@ -179,13 +181,12 @@
             copy = pltpu.make_async_remote_copy(
                 src_ref=part.at[c, pl.ds(pl.multiple_of(peer * SITES, SITES), SITES)],
                 dst_ref=got.at[c, i],
-                send_sem=rs_send.at[c, i],
-                recv_sem=rs_recv.at[c, i],
+                send_sem=rs_send.at[c],
+                recv_sem=rs_recv.at[c],
                 device_id={"gx": peer},
                 device_id_type=pl.DeviceIdType.MESH,
             )
             copy.start()
-            sends.append(copy)
 
     lane = lax.broadcasted_iota(jnp.int32, (8, LANES), 1)
     low = lane < LANES // 2
@@ -208,7 +209,7 @@
             copy = pltpu.make_async_remote_copy(
                 src_ref=blocks.at[k],
                 dst_ref=faces.at[k, back],
-                send_sem=face_send.at[k, i],
+                send_sem=face_send.at[k],
                 recv_sem=face_recv.at[k, back],
                 device_id=neighbours[i],
                 device_id_type=pl.DeviceIdType.MESH,
@@ -266,15 +267,15 @@
                 result.append(new)
         for r in range(RHS):
             blocks[k + 1, r] = packed[r * SITES : (r + 1) * SITES, :].astype(BF16)
-        return result, copies
+        return result
 
     mine = pl.ds(pl.multiple_of(me * SITES, SITES), SITES)
     values = []
     loads[4].wait()
     for c in range(CHUNKS):
         total = part32[c, mine, :]
+        await_bytes(got.at[c], rs_recv.at[c])
         for i in range(len(order)):
-            sends[c * len(order) + i].wait_recv()
             total = total + got[c, i].astype(F32)
         for j in range(PER):
             rounded = total[:, j * LANES : (j + 1) * LANES].astype(BF16)
@@ -282,28 +283,26 @@
             values.append(rounded.astype(F32))
     expand(values, 5)
     sites = [site_rows(5, s) for s in range(SITES)]
-    sites, faces_a = apply_operator(0, sites)
-    sites, faces_b = apply_operator(1, sites)
-
-    gathers = []
+    sites = apply_operator(0, sites)
+    apply_operator(1, sites)
+
     for c in range(CHUNKS):
         for i, (dz, dy) in enumerate(order):
             copy = pltpu.make_async_remote_copy(
                 src_ref=blocks.at[2, pl.ds(c * PER, PER)],
                 dst_ref=whole.at[pl.ds(c * PER, PER), mine],
-                send_sem=ag_send.at[c, i],
-                recv_sem=ag_recv.at[c, i],
+                send_sem=ag_send.at[c],
+                recv_sem=ag_recv.at[c],
                 device_id={"gx": member(dz, dy)},
                 device_id_type=pl.DeviceIdType.MESH,
             )
             copy.start()
-            gathers.append(copy)
-    for r in range(RHS):
-        whole[r, mine, :] = blocks[2, r]
-
-    for c in range(CHUNKS):
-        for i in range(len(order)):
-            gathers[c * len(order) + i].wait_recv()
+        pltpu.make_async_copy(
+            blocks.at[2, pl.ds(c * PER, PER)], whole.at[pl.ds(c * PER, PER), mine], ag_recv.at[c]
+        ).start()
+
+    for c in range(CHUNKS):
+        await_bytes(whole.at[pl.ds(c * PER, PER)], ag_recv.at[c])
         for j in range(PER):
             picked[j] = lax.dot_general(whole[c * PER + j], hot[...], TN, preferred_element_type=F32)
 
@@ -332,8 +331,11 @@
                 out[ri, chi, a] = out32[(ri * 2 + chi) * SC + a].astype(BF16)
     store = pltpu.make_async_copy(out, out_hbm, out_sem)
     store.start()
-    for copy in sends + faces_a + faces_b + gathers:
-        copy.wait_send()
+    for c in range(CHUNKS):
+        await_bytes(got.at[c], rs_send.at[c])
+        await_bytes(whole.at[pl.ds(c * PER, PER), pl.ds(0, groups - SITES)], ag_send.at[c])
+    for k in range(2):
+        await_bytes(faces.at[k], face_send.at[k])
     store.wait()
 
 
@@ -349,7 +351,7 @@
     return pl.pallas_call(
         functools.partial(kernel, nx, nz),
         out_shape=jax.ShapeDtypeStruct(fine_field.shape, BF16),
-        in_specs=[anywhere] * 4,
+        in_specs=[pl.BlockSpec(memory_space=pltpu.HBM)] * 4,
         out_specs=anywhere,
         scratch_shapes=[
             pltpu.VMEM((1, fine), jnp.int32),
@@ -372,15 +374,15 @@
             pltpu.VMEM(fine_field.shape, BF16),
             dma((5,)),
             dma,
-            dma((CHUNKS, peers)),
-            dma((CHUNKS, peers)),
+            dma((CHUNKS,)),
+            dma((CHUNKS,)),
+            dma((2,)),
             dma((2, 5)),
-            dma((2, 5)),
-            dma((CHUNKS, peers)),
-            dma((CHUNKS, peers)),
+            dma((CHUNKS,)),
+            dma((CHUNKS,)),
         ],
         compiler_params=pltpu.CompilerParams(
-            collective_id=0, has_side_effects=True, vmem_limit_bytes=48 * 1024 * 1024
+            collective_id=0, has_side_effects=True
         ),
         name="coarse_cycle",
     )(aggregate.reshape(1, fine), fine_field, null_vectors, coarse_links)

time: 43.6 us -> 38.8 us (0.89)
  local copies, waits for them, and re-layouts: 5.36 us -> 1.68 us
  Pallas kernels: 38 us -> 37 us
    unnamed x9 -> x1, local copies, waits for them, and re-layouts: 5.36 us -> 1.68 us
    pallas_call x1, Pallas kernels: 38 us -> 37 us  [per_device(): pl.pallas_call(functools.partial(kernel, nx, nz), out_shape=jax.ShapeDtyp...]
where the time goes in v1:
time: 38.8 us; the launch traced here: 38.7 us
  Pallas kernels  37 us (95%)
  local copies, waits for them, and re-layouts  1.68 us (4%)
    pallas_call x1, Pallas kernels, per_device(): pl.pallas_call(functools.partial(kernel, nx, nz), out_shape=jax.ShapeDtyp...  37 us
    unnamed x1, local copies, waits for them, and re-layouts  1.68 us

profile of v1, /device:TPU:8, one launch (start us, length us, event | category | flops | bytes accessed | tf_op | source)
XLA Modules:
  0.0 38.7 jit_solution(3867566298699036674)
XLA Ops:
  0.0 37.0 %coarse_cycle.1 = bf16[2,2,6,4,1024]{4,3,2,1,0:T(4,128)(2,1)} custom-call(s32[1,1024]{1,0:T(1,128)} %bitcast.1, bf16[2,2,6,4,1024]{4,3,2,1,0:T(4,128)(2,1)} %field_hbm.1, bf16[2,2,6,32,1024]{4,3,2,1,0:T(8,128)(2,1)} %vec_hbm.1, bf16[2,2,2,2,9,64,128]{6,5,4,3,2,1,0:T(8,128)(2,1)} %links_hbm.1), custom_call_target="tpu_custom_call" | custom-call | tf_op jit(solution)/shard_map/coarse_cycle/pallas_call | solution.py:351
  37.0 1.7 %copy.6 = bf16[2,2,6,4,1024]{4,3,2,1,0:T(4,128)(2,1)} copy(bf16[2,2,6,4,1024]{4,3,2,1,0:T(4,128)(2,1)} %coarse_cycle.1) | data formatting | bytes 393216

commit v2 on v1

v2 whole, which is shorter than its diff:
```python
import functools

import jax
import jax.numpy as jnp
from jax import lax
from jax.experimental import pallas as pl
from jax.experimental.pallas import tpu as pltpu
from jax.sharding import PartitionSpec as P

RHS = 4
NV = 32
SC = 6
SITES = 16
LANES = 128
BACK = (1, 0, 3, 2, 4)
FAR_FIRST = (2, 3, 0, 1, 4)
F32 = jnp.float32
BF16 = jnp.bfloat16
NT = (((1,), (1,)), ((), ()))
TN = (((0,), (0,)), ((), ()))


def ring_order(count):
    long = count // 2
    pairs = [(dz, dy) for dz in range(long) for dy in range(2) if (dz, dy) != (0, 0)]
    return sorted(pairs, key=lambda p: -(2 * min(p[0], long - p[0]) + p[1]))


def site_bits(s):
    return (s >> 3) & 1, (s >> 2) & 1, (s >> 1) & 1, s & 1


def site_of(x, y, z, t):
    return ((x * 2 + y) * 2 + z) * 2 + t


def local_terms(s):
    x, y, z, t = site_bits(s)
    return (
        (0, s),
        (1, site_of(x, 1 - y, z, t)),
        (2, site_of(x, 1 - y, z, t)),
        (3 if x == 0 else 4, site_of(1 - x, y, z, t)),
        (5 if z == 0 else 6, site_of(x, y, 1 - z, t)),
        (7 if t == 0 else 8, site_of(x, y, z, 1 - t)),
    )


def remote_terms(s):
    x, y, z, t = site_bits(s)
    return (
        (3, 0, site_of(0, y, z, t)) if x == 1 else (4, 1, site_of(1, y, z, t)),
        (5, 2, site_of(x, y, 0, t)) if z == 1 else (6, 3, site_of(x, y, 1, t)),
        (7, 4, site_of(x, y, z, 0)) if t == 1 else (8, 4, site_of(x, y, z, 1)),
    )


def kernel(
    nx,
    nz,
    agg_hbm,
    field_hbm,
    vec_hbm,
    links_hbm,
    out,
    agg,
    field,
    field32,
    vec,
    links,
    hot,
    rows,
    part,
    got,
    spread,
    faces,
    blocks,
    packed,
    whole,
    picked,
    in_sem,
    rs_send,
    rs_recv,
    face_send,
    face_recv,
    ag_send,
    ag_recv,
):
    def await_bytes(ref, sem):
        pltpu.make_async_copy(ref, ref, sem).wait()

    fine = agg.shape[1]
    tiles = fine // LANES
    me = lax.axis_index("gx")
    my_z = lax.axis_index("gz")
    my_t = lax.axis_index("ta")
    order = ring_order(nx)
    long = nx // 2

    loads = [
        pltpu.make_async_copy(agg_hbm, agg, in_sem.at[0]),
        pltpu.make_async_copy(field_hbm, field, in_sem.at[1]),
        pltpu.make_async_copy(vec_hbm.at[:, 0], vec.at[:, 0], in_sem.at[2]),
        pltpu.make_async_copy(vec_hbm.at[:, 1], vec.at[:, 1], in_sem.at[3]),
        pltpu.make_async_copy(links_hbm, links, in_sem.at[4]),
    ]
    for load in loads[:4]:
        load.start()

    def member(dz, dy):
        z = lax.rem(lax.div(me, 2) + dz, long)
        y = lax.rem(lax.rem(me, 2) + dy, 2)
        return z * 2 + y

    barrier = pltpu.get_barrier_semaphore()
    neighbours = [
        {"gx": lax.rem(me + 1, nx)},
        {"gx": lax.rem(me + nx - 1, nx)},
        {"gz": lax.rem(my_z + 1, nz)},
        {"gz": lax.rem(my_z + nz - 1, nz)},
        {"ta": 1 - my_t},
    ]
    greeted = [{"gx": member(dz, dy)} for dz, dy in order] + neighbours[2:]
    for device in greeted:
        pl.semaphore_signal(barrier, inc=1, device_id=device, device_id_type=pl.DeviceIdType.MESH)

    loads[0].wait()
    groups = hot.shape[0]

    def hot_tile(i, carry):
        lanes = pl.ds(pl.multiple_of(i * LANES, LANES), LANES)
        site = lax.broadcasted_iota(jnp.int32, (groups, LANES), 0)
        hot[:, lanes] = jnp.where(site == agg[:, lanes], 1.0, 0.0).astype(BF16)
        return carry

    lax.fori_loop(0, tiles, hot_tile, 0)

    loads[1].wait()
    for chi in range(2):
        for a in range(SC):
            plane = chi * SC + a
            fr = field[0, chi, a].astype(F32)
            fi = field[1, chi, a].astype(F32)
            field32[plane] = fr
            field32[2 * SC + plane] = fi
            field32[4 * SC + plane] = fr + fi
    loads[2].wait()
    loads[3].wait()

    loads[4].start()

    def project(step, carry):
        chi = lax.div(step, tiles)
        lanes = pl.ds(pl.multiple_of(lax.rem(step, tiles) * LANES, LANES), LANES)
        height = NV // 2
        for part_of in range(2):
            zero = jnp.zeros((height, LANES), F32)
            both, less, more = [zero] * RHS, [zero] * RHS, [zero] * RHS
            for a in range(SC):
                plane = chi * SC + a
                vr = vec[0, chi, a, part_of * height : (part_of + 1) * height, lanes].astype(F32)
                vi = vec[1, chi, a, part_of * height : (part_of + 1) * height, lanes].astype(F32)
                diff, total = vr - vi, vr + vi
                for r in range(RHS):
                    fr = field32[plane, r : r + 1, lanes]
                    fi = field32[2 * SC + plane, r : r + 1, lanes]
                    fs = field32[4 * SC + plane, r : r + 1, lanes]
                    both[r] = both[r] + vr * fs
                    less[r] = less[r] + diff * fi
                    more[r] = more[r] + total * fr
            base = pl.multiple_of(chi * NV + part_of * height, height)
            for r in range(RHS):
                rows[pl.ds(r * LANES + base, height), lanes] = (both[r] - less[r]).astype(BF16)
                rows[pl.ds(r * LANES + 2 * NV + base, height), lanes] = (both[r] - more[r]).astype(BF16)
        return carry

    lax.fori_loop(0, 2 * tiles, project, 0)
    part[...] = lax.dot_general(hot[...], rows[...], NT, preferred_element_type=F32).astype(BF16)
    pl.semaphore_wait(barrier, len(greeted))
    for i, (dz, dy) in enumerate(order):
        peer = member(dz, dy)
        pltpu.make_async_remote_copy(
            src_ref=part.at[pl.ds(pl.multiple_of(peer * SITES, SITES), SITES)],
            dst_ref=got.at[i],
            send_sem=rs_send,
            recv_sem=rs_recv,
            device_id={"gx": peer},
            device_id_type=pl.DeviceIdType.MESH,
        ).start()

    lane = lax.broadcasted_iota(jnp.int32, (8, LANES), 1)
    low = lane < LANES // 2
    low16 = lax.broadcasted_iota(jnp.int32, (SITES, LANES), 1) < LANES // 2
    upper = lax.broadcasted_iota(jnp.int32, (8, LANES), 0) < RHS
    half = LANES // 2

    def expand(values, slot):
        for r in range(RHS):
            v = values[r]
            spread[slot, r * SITES : (r + 1) * SITES, :] = jnp.where(low16, v, -v)
            spread[slot, (RHS + r) * SITES : (RHS + r + 1) * SITES, :] = pltpu.roll(v, half, 1)

    def site_rows(slot, s):
        return spread[slot, pl.ds(s, 2 * RHS, stride=SITES), :]

    def send_faces(k):
        copies = {}
        for i in FAR_FIRST:
            back = BACK[i]
            copy = pltpu.make_async_remote_copy(
                src_ref=blocks.at[k],
                dst_ref=faces.at[k, back],
                send_sem=face_send.at[k],
                recv_sem=face_recv.at[k, back],
                device_id=neighbours[i],
                device_id_type=pl.DeviceIdType.MESH,
            )
            copy.start()
            copies[back] = copy
        return copies

    def term_product(group, terms):
        total = None
        count = len(terms[0])
        for first in range(0, count, 2):
            pick = range(first, min(first + 2, count))
            left = [jnp.concatenate([terms[j][m][1] for j in range(4)], axis=0).astype(BF16) for m in pick]
            right = []
            for m in pick:
                part_links = []
                for j in range(4):
                    x, y, z, t = site_bits(group * 4 + j)
                    part_links.append(links[x, y, z, t, terms[j][m][0]])
                right.append(jnp.concatenate(part_links, axis=0))
            lhs = left[0] if len(left) == 1 else jnp.concatenate(left, axis=1)
            rhs = right[0] if len(right) == 1 else jnp.concatenate(right, axis=1)
            product = lax.dot_general(lhs, rhs, NT, preferred_element_type=F32)
            total = product if total is None else total + product
        return total

    def apply_operator(k, sites):
        copies = send_faces(k)
        totals = []
        for group in range(4):
            terms = [[(m, sites[n]) for m, n in local_terms(group * 4 + j)] for j in range(4)]
            totals.append(term_product(group, terms))
        for slots, which in (((4, 0, 1), (0, 2)), ((2, 3), (1,))):
            for slot in slots:
                copies[slot].wait_recv()
                block = faces[k, slot].astype(F32)
                expand([block[:, r * LANES : (r + 1) * LANES] for r in range(RHS)], slot)
            for group in range(4):
                terms = []
                for j in range(4):
                    remote = remote_terms(group * 4 + j)
                    terms.append([(remote[w][0], site_rows(remote[w][1], remote[w][2])) for w in which])
                totals[group] = totals[group] + term_product(group, terms)
        result = []
        for group in range(4):
            total = totals[group]
            for j in range(4):
                block = total[8 * j : 8 * j + 8, LANES * (j // 2) : LANES * (j // 2) + LANES]
                swapped = pltpu.roll(block, RHS, 0)
                signed = jnp.where(upper, -swapped, swapped)
                if j % 2 == 0:
                    new = jnp.where(low, block, pltpu.roll(signed, half, 1))
                else:
                    new = jnp.where(low, pltpu.roll(block, half, 1), signed)
                new = new.astype(BF16).astype(F32)
                s = group * 4 + j
                kept = jnp.where(low, new, -new)
                packed[pl.ds(s, RHS, stride=SITES), :] = kept[:RHS]
                result.append(new)
        for r in range(RHS):
            blocks[k + 1, :, r * LANES : (r + 1) * LANES] = packed[r * SITES : (r + 1) * SITES, :].astype(BF16)
        return result

    mine = pl.ds(pl.multiple_of(me * SITES, SITES), SITES)
    values = []
    loads[4].wait()
    await_bytes(got, rs_recv)
    for r in range(RHS):
        lanes = slice(r * LANES, (r + 1) * LANES)
        total = part[mine, lanes].astype(F32)
        for i in range(len(order)):
            total = total + got[i, :, lanes].astype(F32)
        rounded = total.astype(BF16)
        blocks[0, :, lanes] = rounded
        values.append(rounded.astype(F32))
    expand(values, 5)
    sites = [site_rows(5, s) for s in range(SITES)]
    sites = apply_operator(0, sites)
    apply_operator(1, sites)

    for dz, dy in order:
        pltpu.make_async_remote_copy(
            src_ref=blocks.at[2],
            dst_ref=whole.at[mine],
            send_sem=ag_send,
            recv_sem=ag_recv,
            device_id={"gx": member(dz, dy)},
            device_id_type=pl.DeviceIdType.MESH,
        ).start()
    pltpu.make_async_copy(blocks.at[2], whole.at[mine], ag_recv).start()

    depth = 2 * NV * RHS
    row = lax.broadcasted_iota(jnp.int32, (2 * RHS, depth), 0)
    column = lax.broadcasted_iota(jnp.int32, (2 * RHS, depth), 1)
    wanted = (column >> 6) + ((column >> 5) & 1) * RHS
    signs = jnp.where(row == wanted, 1.0, 0.0).astype(BF16)

    await_bytes(whole, ag_recv)
    picked[...] = lax.dot_general(whole[...], hot[...], TN, preferred_element_type=F32).astype(BF16)
    wide = 2 * LANES
    steps = fine // wide

    def prolong(step, carry):
        chi = lax.div(step, steps)
        lanes = pl.ds(pl.multiple_of(lax.rem(step, steps) * wide, wide), wide)
        base = pl.multiple_of(chi * NV, NV)
        pr = [picked[pl.ds(r * LANES + base, NV), lanes] for r in range(RHS)]
        pi = [picked[pl.ds(r * LANES + 2 * NV + base, NV), lanes] for r in range(RHS)]
        for a in range(SC):
            vr = vec[0, chi, a, :, lanes]
            vi = vec[1, chi, a, :, lanes]
            products = []
            for r in range(RHS):
                products += [vr * pr[r] - vi * pi[r], vr * pi[r] + vi * pr[r]]
            both = jnp.dot(signs, jnp.concatenate(products, axis=0), preferred_element_type=F32)
            out[0, chi, a, :, lanes] = both[:RHS].astype(BF16)
            out[1, chi, a, :, lanes] = both[RHS:].astype(BF16)
        return carry

    lax.fori_loop(0, 2 * steps, prolong, 0)
    await_bytes(got, rs_send)
    await_bytes(whole.at[pl.ds(0, groups - SITES)], ag_send)
    for k in range(2):
        await_bytes(faces.at[k], face_send.at[k])


def per_device(fine_field, null_vectors, aggregate, coarse_links):
    nx = lax.axis_size("gx")
    nz = lax.axis_size("gz")
    fine = fine_field.shape[-1]
    groups = SITES * nx
    peers = nx - 1
    width = RHS * LANES
    dma = pltpu.SemaphoreType.DMA
    return pl.pallas_call(
        functools.partial(kernel, nx, nz),
        out_shape=jax.ShapeDtypeStruct(fine_field.shape, BF16),
        in_specs=[pl.BlockSpec(memory_space=pltpu.HBM)] * 4,
        out_specs=pl.BlockSpec(memory_space=pltpu.VMEM),
        scratch_shapes=[
            pltpu.VMEM((1, fine), jnp.int32),
            pltpu.VMEM(fine_field.shape, BF16),
            pltpu.VMEM((6 * SC, RHS, fine), F32),
            pltpu.VMEM(null_vectors.shape, BF16),
            pltpu.VMEM(coarse_links.shape, BF16),
            pltpu.VMEM((groups, fine), BF16),
            pltpu.VMEM((width, fine), BF16),
            pltpu.VMEM((groups, width), BF16),
            pltpu.VMEM((peers, SITES, width), BF16),
            pltpu.VMEM((6, 2 * RHS * SITES, LANES), F32),
            pltpu.VMEM((2, 5, SITES, RHS * LANES), BF16),
            pltpu.VMEM((3, SITES, RHS * LANES), BF16),
            pltpu.VMEM((RHS * SITES, LANES), F32),
            pltpu.VMEM((groups, RHS * LANES), BF16),
            pltpu.VMEM((RHS * LANES, fine), BF16),
            dma((5,)),
            dma,
            dma,
            dma((2,)),
            dma((2, 5)),
            dma,
            dma,
        ],
        compiler_params=pltpu.CompilerParams(
            collective_id=0, has_side_effects=True, vmem_limit_bytes=48 * 1024 * 1024
        ),
        name="coarse_cycle",
    )(*[pltpu.with_memory_space_constraint(v, pltpu.HBM) for v in (aggregate.reshape(1, fine), fine_field, null_vectors, coarse_links)])


def solution(mesh):
    in_specs = (
        P(None, None, None, None, ("gx", "gz", "ta")),
        P(None, None, None, None, ("gx", "gz", "ta")),
        P(("gx", "gz", "ta")),
        P("gx", None, "gz", "ta", None, None, None),
    )
    out_specs = P(None, None, None, None, ("gx", "gz", "ta"))
    return jax.shard_map(per_device, mesh=mesh, in_specs=in_specs, out_specs=out_specs, check_vma=False)
```

time: 38.8 us -> 36.3 us (0.936)
  Pallas kernels: 37 us -> 35.5 us
  local copies, waits for them, and re-layouts: 1.68 us -> 0.68 us
    pallas_call x1, Pallas kernels: 37 us -> 35.5 us  [per_device(): pl.pallas_call(functools.partial(kernel, nx, nz), out_shape=jax.ShapeDtyp...]
    unnamed x1, local copies, waits for them, and re-layouts: 1.68 us -> 0.68 us
where the time goes in v2:
time: 36.3 us; the launch traced here: 36.2 us
  Pallas kernels  35.5 us (98%)
  local copies, waits for them, and re-layouts  0.68 us (2%)
    pallas_call x1, Pallas kernels, per_device(): pl.pallas_call(functools.partial(kernel, nx, nz), out_shape=jax.ShapeDtyp...  35.5 us

profile of v2, /device:TPU:8, one launch (start us, length us, event | category | flops | bytes accessed | tf_op | source)
XLA Modules:
  0.0 36.2 jit_solution(6526744714882367285)
XLA Ops:
  0.0 35.5 %coarse_cycle.1 = bf16[2,2,6,4,1024]{4,3,2,1,0:T(4,128)(2,1)S(1)} custom-call(s32[1,1024]{1,0:T(1,128)} %bitcast.1, bf16[2,2,6,4,1024]{4,3,2,1,0:T(4,128)(2,1)} %field_hbm.1, bf16[2,2,6,32,1024]{4,3,2,1,0:T(8,128)(2,1)} %vec_hbm.1, bf16[2,2,2,2,9,64,128]{6,5,4,3,2,1,0:T(8,128)(2,1)} %links_hbm.1), custom_call_target="tpu_custom_call" | custom-call | tf_op jit(solution)/shard_map/coarse_cycle/pallas_call | solution.py:349
  35.5 0.7 %copy.6 = bf16[2,2,6,4,1024]{4,3,2,1,0:T(4,128)(2,1)} copy(bf16[2,2,6,4,1024]{4,3,2,1,0:T(4,128)(2,1)S(1)} %coarse_cycle.1) | data formatting | bytes 393216

commit v3 on v2

--- a/solution.py
+++ b/solution.py
@@ -331,7 +331,7 @@
             out[1, chi, a, :, lanes] = both[RHS:].astype(BF16)
         return carry
 
-    lax.fori_loop(0, 2 * steps, prolong, 0)
+    lax.fori_loop(0, 2 * steps, prolong, 0, unroll=4)
     await_bytes(got, rs_send)
     await_bytes(whole.at[pl.ds(0, groups - SITES)], ag_send)
     for k in range(2):

time: 36.3 us -> 35.5 us (0.978)
  Pallas kernels: 35.5 us -> 34.8 us
    pallas_call x1, Pallas kernels: 35.5 us -> 34.8 us  [per_device(): pl.pallas_call(functools.partial(kernel, nx, nz), out_shape=jax.ShapeDtyp...]
where the time goes in v3:
time: 35.5 us; the launch traced here: 35.4 us
  Pallas kernels  34.8 us (98%)
  local copies, waits for them, and re-layouts  0.68 us (2%)
    pallas_call x1, Pallas kernels, per_device(): pl.pallas_call(functools.partial(kernel, nx, nz), out_shape=jax.ShapeDtyp...  34.8 us

profile of v3, /device:TPU:8, one launch (start us, length us, event | category | flops | bytes accessed | tf_op | source)
XLA Modules:
  0.0 35.4 jit_solution(13245084716448164467)
XLA Ops:
  0.0 34.8 %coarse_cycle.1 = bf16[2,2,6,4,1024]{4,3,2,1,0:T(4,128)(2,1)S(1)} custom-call(s32[1,1024]{1,0:T(1,128)} %bitcast.1, bf16[2,2,6,4,1024]{4,3,2,1,0:T(4,128)(2,1)} %field_hbm.1, bf16[2,2,6,32,1024]{4,3,2,1,0:T(8,128)(2,1)} %vec_hbm.1, bf16[2,2,2,2,9,64,128]{6,5,4,3,2,1,0:T(8,128)(2,1)} %links_hbm.1), custom_call_target="tpu_custom_call" | custom-call | tf_op jit(solution)/shard_map/coarse_cycle/pallas_call | solution.py:349
  34.8 0.7 %copy.6 = bf16[2,2,6,4,1024]{4,3,2,1,0:T(4,128)(2,1)} copy(bf16[2,2,6,4,1024]{4,3,2,1,0:T(4,128)(2,1)S(1)} %coarse_cycle.1) | data formatting | bytes 393216

commit v4 on v3

--- a/solution.py
+++ b/solution.py
@@ -62,13 +62,13 @@
     field_hbm,
     vec_hbm,
     links_hbm,
-    out,
+    whole,
+    vec,
+    hot,
     agg,
     field,
     field32,
-    vec,
     links,
-    hot,
     rows,
     part,
     got,
@@ -76,8 +76,6 @@
     faces,
     blocks,
     packed,
-    whole,
-    picked,
     in_sem,
     rs_send,
     rs_recv,
@@ -303,13 +301,21 @@
         ).start()
     pltpu.make_async_copy(blocks.at[2], whole.at[mine], ag_recv).start()
 
+    await_bytes(whole, ag_recv)
+    await_bytes(got, rs_send)
+    await_bytes(whole.at[pl.ds(0, groups - SITES)], ag_send)
+    for k in range(2):
+        await_bytes(faces.at[k], face_send.at[k])
+
+
+def prolong_kernel(whole, vec, hot, out_hbm, picked, out, sem):
+    fine = hot.shape[1]
     depth = 2 * NV * RHS
     row = lax.broadcasted_iota(jnp.int32, (2 * RHS, depth), 0)
     column = lax.broadcasted_iota(jnp.int32, (2 * RHS, depth), 1)
     wanted = (column >> 6) + ((column >> 5) & 1) * RHS
     signs = jnp.where(row == wanted, 1.0, 0.0).astype(BF16)
 
-    await_bytes(whole, ag_recv)
     picked[...] = lax.dot_general(whole[...], hot[...], TN, preferred_element_type=F32).astype(BF16)
     wide = 2 * LANES
     steps = fine // wide
@@ -331,11 +337,18 @@
             out[1, chi, a, :, lanes] = both[RHS:].astype(BF16)
         return carry
 
-    lax.fori_loop(0, 2 * steps, prolong, 0, unroll=4)
-    await_bytes(got, rs_send)
-    await_bytes(whole.at[pl.ds(0, groups - SITES)], ag_send)
-    for k in range(2):
-        await_bytes(faces.at[k], face_send.at[k])
+    stores = []
+    for i in range(steps):
+        for chi in range(2):
+            prolong(chi * steps + i, 0)
+        lanes = pl.ds(i * wide, wide)
+        store = pltpu.make_async_copy(
+            out.at[:, :, :, :, lanes], out_hbm.at[:, :, :, :, lanes], sem.at[i]
+        )
+        store.start()
+        stores.append(store)
+    for store in stores:
+        store.wait()
 
 
 def per_device(fine_field, null_vectors, aggregate, coarse_links):
@@ -346,18 +359,21 @@
     peers = nx - 1
     width = RHS * LANES
     dma = pltpu.SemaphoreType.DMA
-    return pl.pallas_call(
+    vmem = pl.BlockSpec(memory_space=pltpu.VMEM)
+    whole, vec, hot = pl.pallas_call(
         functools.partial(kernel, nx, nz),
-        out_shape=jax.ShapeDtypeStruct(fine_field.shape, BF16),
+        out_shape=(
+            jax.ShapeDtypeStruct((groups, width), BF16),
+            jax.ShapeDtypeStruct(null_vectors.shape, BF16),
+            jax.ShapeDtypeStruct((groups, fine), BF16),
+        ),
         in_specs=[pl.BlockSpec(memory_space=pltpu.HBM)] * 4,
-        out_specs=pl.BlockSpec(memory_space=pltpu.VMEM),
+        out_specs=(vmem, vmem, vmem),
         scratch_shapes=[
             pltpu.VMEM((1, fine), jnp.int32),
             pltpu.VMEM(fine_field.shape, BF16),
             pltpu.VMEM((6 * SC, RHS, fine), F32),
-            pltpu.VMEM(null_vectors.shape, BF16),
             pltpu.VMEM(coarse_links.shape, BF16),
-            pltpu.VMEM((groups, fine), BF16),
             pltpu.VMEM((width, fine), BF16),
             pltpu.VMEM((groups, width), BF16),
             pltpu.VMEM((peers, SITES, width), BF16),
@@ -365,8 +381,6 @@
             pltpu.VMEM((2, 5, SITES, RHS * LANES), BF16),
             pltpu.VMEM((3, SITES, RHS * LANES), BF16),
             pltpu.VMEM((RHS * SITES, LANES), F32),
-            pltpu.VMEM((groups, RHS * LANES), BF16),
-            pltpu.VMEM((RHS * LANES, fine), BF16),
             dma((5,)),
             dma,
             dma,
@@ -380,6 +394,19 @@
         ),
         name="coarse_cycle",
     )(*[pltpu.with_memory_space_constraint(v, pltpu.HBM) for v in (aggregate.reshape(1, fine), fine_field, null_vectors, coarse_links)])
+    return pl.pallas_call(
+        prolong_kernel,
+        out_shape=jax.ShapeDtypeStruct(fine_field.shape, BF16),
+        in_specs=[vmem] * 3,
+        out_specs=pl.BlockSpec(memory_space=pltpu.HBM),
+        scratch_shapes=[
+            pltpu.VMEM((RHS * LANES, fine), BF16),
+            pltpu.VMEM(fine_field.shape, BF16),
+            dma((fine // (2 * LANES),)),
+        ],
+        compiler_params=pltpu.CompilerParams(vmem_limit_bytes=48 * 1024 * 1024),
+        name="prolong",
+    )(whole, vec, hot)
 
 
 def solution(mesh):

time: 35.5 us -> 35.3 us (level)
  local copies, waits for them, and re-layouts: 0.68 us -> 0 us
  Pallas kernels: 34.8 us -> 35.2 us
    unnamed x1 -> x0, local copies, waits for them, and re-layouts: 0.68 us -> none
    pallas_call x1 -> x2, Pallas kernels: 34.8 us -> 35.2 us  [the longest x1 33.2 us: per_device(): pl.pallas_call(functools.partial(kernel, nx, nz), out_shape=(jax.ShapeDty...]
where the time goes in v4:
time: 35.3 us; the launch traced here: 35.2 us
  Pallas kernels  35.2 us (100%)
    pallas_call x1, Pallas kernels, per_device(): pl.pallas_call(functools.partial(kernel, nx, nz), out_shape=(jax.ShapeDty...  33.2 us
    pallas_call x1, Pallas kernels, per_device(): pl.pallas_call(prolong_kernel, out_shape=jax.ShapeDtypeStruct(fine_field....  2.02 us

profile of v4, /device:TPU:8, one launch (start us, length us, event | category | flops | bytes accessed | tf_op | source)
XLA Modules:
  0.0 35.2 jit_solution(9354035019759172397)
XLA Ops:
  0.0 33.2 %coarse_cycle.1 = (bf16[256,512]{1,0:T(8,128)(2,1)S(1)}, bf16[2,2,6,32,1024]{4,3,2,1,0:T(8,128)(2,1)S(1)}, bf16[256,1024]{1,0:T(8,128)(2,1)S(1)}) custom-call(s32[1,1024]{1,0:T(1,128)} %bitcast.1, bf16[2,2,6,4,1024]{4,3,2,1,0:T(4,128)(2,1)} %field_hbm.1, bf16[2,2,6,32,1024]{4,3,2,1,0:T(8,128)(2,1)} %vec_hbm.1, bf16[2,2,2,2,9,64,128]{6,5,4,3,2,1,0:T(8,128)(2,1)} %links_hbm.1), custom_call_target="tpu_custom_call" | custom-call | tf_op jit(solution)/shard_map/coarse_cycle/pallas_call | solution.py:363
  33.2 2.0 %prolong.1 = bf16[2,2,6,4,1024]{4,3,2,1,0:T(4,128)(2,1)} custom-call(bf16[256,512]{1,0:T(8,128)(2,1)S(1)} %get-tuple-element.8.whole, bf16[2,2,6,32,1024]{4,3,2,1,0:T(8,128)(2,1)S(1)} %get-tuple-element.9.vec, bf16[256,1024]{1,0:T(8,128)(2,1)S(1)} %get-tuple-element.10.hot), custom_call_target="tpu_custom_call" | custom-call | tf_op jit(solution)/shard_map/prolong/pallas_call | solution.py:397

commit v5 on v4

--- a/solution.py
+++ b/solution.py
@@ -105,9 +105,13 @@
     for load in loads[:4]:
         load.start()
 
+    my_row = lax.div(me, 2)
+    my_side = me - 2 * my_row
+
     def member(dz, dy):
-        z = lax.rem(lax.div(me, 2) + dz, long)
-        y = lax.rem(lax.rem(me, 2) + dy, 2)
+        z = my_row + dz
+        z = jnp.where(z >= long, z - long, z)
+        y = 1 - my_side if dy == 1 else my_side
         return z * 2 + y
 
     barrier = pltpu.get_barrier_semaphore()

time: 35.3 us -> 35.3 us (level)
  no operation moved by 1% of the time
where the time goes in v5:
time: 35.3 us; the launch traced here: 35.2 us
  Pallas kernels  35.2 us (100%)
    pallas_call x1, Pallas kernels, per_device(): pl.pallas_call(functools.partial(kernel, nx, nz), out_shape=(jax.ShapeDty...  33.2 us
    pallas_call x1, Pallas kernels, per_device(): pl.pallas_call(prolong_kernel, out_shape=jax.ShapeDtypeStruct(fine_field....  2.02 us

profile of v5, /device:TPU:8, one launch (start us, length us, event | category | flops | bytes accessed | tf_op | source)
XLA Modules:
  0.0 35.2 jit_solution(8017634851843389587)
XLA Ops:
  0.0 33.2 %coarse_cycle.1 = (bf16[256,512]{1,0:T(8,128)(2,1)S(1)}, bf16[2,2,6,32,1024]{4,3,2,1,0:T(8,128)(2,1)S(1)}, bf16[256,1024]{1,0:T(8,128)(2,1)S(1)}) custom-call(s32[1,1024]{1,0:T(1,128)} %bitcast.1, bf16[2,2,6,4,1024]{4,3,2,1,0:T(4,128)(2,1)} %field_hbm.1, bf16[2,2,6,32,1024]{4,3,2,1,0:T(8,128)(2,1)} %vec_hbm.1, bf16[2,2,2,2,9,64,128]{6,5,4,3,2,1,0:T(8,128)(2,1)} %links_hbm.1), custom_call_target="tpu_custom_call" | custom-call | tf_op jit(solution)/shard_map/coarse_cycle/pallas_call | solution.py:367
  33.2 2.0 %prolong.1 = bf16[2,2,6,4,1024]{4,3,2,1,0:T(4,128)(2,1)} custom-call(bf16[256,512]{1,0:T(8,128)(2,1)S(1)} %get-tuple-element.8.whole, bf16[2,2,6,32,1024]{4,3,2,1,0:T(8,128)(2,1)S(1)} %get-tuple-element.9.vec, bf16[256,1024]{1,0:T(8,128)(2,1)S(1)} %get-tuple-element.10.hot), custom_call_target="tpu_custom_call" | custom-call | tf_op jit(solution)/shard_map/prolong/pallas_call | solution.py:401

commit v6 on v4

--- a/solution.py
+++ b/solution.py
@@ -143,9 +143,6 @@
             field32[2 * SC + plane] = fi
             field32[4 * SC + plane] = fr + fi
     loads[2].wait()
-    loads[3].wait()
-
-    loads[4].start()
 
     def project(step, carry):
         chi = lax.div(step, tiles)
@@ -172,7 +169,10 @@
                 rows[pl.ds(r * LANES + 2 * NV + base, height), lanes] = (both[r] - more[r]).astype(BF16)
         return carry
 
-    lax.fori_loop(0, 2 * tiles, project, 0)
+    lax.fori_loop(0, tiles, project, 0)
+    loads[3].wait()
+    loads[4].start()
+    lax.fori_loop(tiles, 2 * tiles, project, 0)
     part[...] = lax.dot_general(hot[...], rows[...], NT, preferred_element_type=F32).astype(BF16)
     pl.semaphore_wait(barrier, len(greeted))
     for i, (dz, dy) in enumerate(order):

time: 35.3 us -> 35.2 us (level)
  no operation moved by 1% of the time
where the time goes in v6:
time: 35.2 us; the launch traced here: 35.1 us
  Pallas kernels  35.1 us (100%)
    pallas_call x1, Pallas kernels, per_device(): pl.pallas_call(functools.partial(kernel, nx, nz), out_shape=(jax.ShapeDty...  33.1 us
    pallas_call x1, Pallas kernels, per_device(): pl.pallas_call(prolong_kernel, out_shape=jax.ShapeDtypeStruct(fine_field....  2.02 us

profile of v6, /device:TPU:8, one launch (start us, length us, event | category | flops | bytes accessed | tf_op | source)
XLA Modules:
  0.0 35.1 jit_solution(17060013139263922853)
XLA Ops:
  0.0 33.1 %coarse_cycle.1 = (bf16[256,512]{1,0:T(8,128)(2,1)S(1)}, bf16[2,2,6,32,1024]{4,3,2,1,0:T(8,128)(2,1)S(1)}, bf16[256,1024]{1,0:T(8,128)(2,1)S(1)}) custom-call(s32[1,1024]{1,0:T(1,128)} %bitcast.1, bf16[2,2,6,4,1024]{4,3,2,1,0:T(4,128)(2,1)} %field_hbm.1, bf16[2,2,6,32,1024]{4,3,2,1,0:T(8,128)(2,1)} %vec_hbm.1, bf16[2,2,2,2,9,64,128]{6,5,4,3,2,1,0:T(8,128)(2,1)} %links_hbm.1), custom_call_target="tpu_custom_call" | custom-call | tf_op jit(solution)/shard_map/coarse_cycle/pallas_call | solution.py:363
  33.1 2.0 %prolong.1 = bf16[2,2,6,4,1024]{4,3,2,1,0:T(4,128)(2,1)} custom-call(bf16[256,512]{1,0:T(8,128)(2,1)S(1)} %get-tuple-element.8.whole, bf16[2,2,6,32,1024]{4,3,2,1,0:T(8,128)(2,1)S(1)} %get-tuple-element.9.vec, bf16[256,1024]{1,0:T(8,128)(2,1)S(1)} %get-tuple-element.10.hot), custom_call_target="tpu_custom_call" | custom-call | tf_op jit(solution)/shard_map/prolong/pallas_call | solution.py:397
